TPU v7x, 256 devices: a whole 4x4x8 slice. The times are simulated.
256 devices in a mesh: snap: 32 (over z_hi, x, y), vert: 8 (over z_lo, core).
Axes of the slice: x: 4, y: 4, z: 8 (z_hi: 2, z_lo: 4; z = z_hi * 4 + z_lo), core: 2. Of those that a mesh axis runs over, the one named last changes fastest.
Arguments:
- features: bfloat16 [64, 8192, 128], P('snap', 'vert'), may hold values from -6 to 6
- tile_cols: int32 [64, 64, 8], P('snap', 'vert'), may hold values from 0 to 63
- tile_weights: int32 [64, 64, 8, 128, 128], P('snap', 'vert'), may hold values from 0 to 3
- graph_gain: float32 [2, 128], replicated, may hold values from 0.5 to 1.5
- graph_up: bfloat16 [2, 128, 512], replicated, may hold values from -0.5 to 0.5
- graph_down: bfloat16 [2, 512, 128], replicated, may hold values from -0.25 to 0.25
- lag_mix: float32 [2, 8, 128], replicated, may hold values from -2 to 2
- time_gain: float32 [2, 128], replicated, may hold values from 0.5 to 1.5
- time_up: bfloat16 [2, 128, 1024], replicated, may hold values from -0.5 to 0.5
- time_down: bfloat16 [2, 1024, 128], replicated, may hold values from -0.1875 to 0.1875
Outputs:
- result: bfloat16 [64, 8192, 128], P('snap', 'vert')
All inputs are finite; a program needn't handle non-finite values.
Results may differ from a plain program's by a relative error of at most 0.0085.
Values may be sent and summed in bfloat16 or wider, within the bound.
No kernel may reach another device: no remote copies, remote signals or barrier semaphores. Data moves between devices by JAX's collectives and lax.ppermute only.
A program may use at most 64 MiB of HBM per device.

v0:
```python
import jax
import jax.numpy as jnp
from jax import lax
from jax.sharding import PartitionSpec as P

eps = 1e-06


def rms_scale(activation, gain_row):
    return (
        activation
        * lax.rsqrt(jnp.mean(activation * activation, axis=-1, keepdims=True) + eps)
        * gain_row
    )


def mlp_branch(residual, mixed_rows, gain_row, up_weight, down_weight):
    feature_width = residual.shape[-1]
    normed = rms_scale(mixed_rows, gain_row).astype(jnp.bfloat16).reshape(-1, feature_width)
    hidden = jax.nn.gelu(jnp.dot(normed, up_weight, preferred_element_type=jnp.float32)).astype(
        jnp.bfloat16
    )
    branch = jnp.dot(hidden, down_weight, preferred_element_type=jnp.float32).reshape(
        residual.shape
    )
    return (residual.astype(jnp.float32) + branch).astype(jnp.bfloat16)


def lagged(sequence, lag_rows, before, out_count):
    widened = sequence.astype(jnp.float32)
    running = jnp.zeros((out_count,) + sequence.shape[1:], jnp.float32)
    for lag_step in range(lag_rows.shape[0]):
        running = running + lag_rows[lag_step] * lax.slice_in_dim(
            widened, before - lag_step, before - lag_step + out_count, axis=0
        )
    return running


def aggregate(snapshot, columns, blocks):
    tile_size = blocks.shape[-1]
    feature_width = snapshot.shape[-1]
    stacked = snapshot.reshape(-1, tile_size, feature_width)
    picked = stacked[columns]
    product = jnp.einsum("rkij,rkjf->rif", blocks, picked, preferred_element_type=jnp.float32)
    return product.reshape(-1, feature_width)


def on_device(
    features,
    tile_cols,
    tile_weights,
    graph_gain,
    graph_up,
    graph_down,
    lag_mix,
    time_gain,
    time_up,
    time_down,
):
    blocks = tile_weights.astype(jnp.bfloat16)
    state = features
    owners = lax.axis_size("snap")
    snap_dev, vert_dev, feature_width = features.shape
    lag_count = lag_mix.shape[1]
    for layer_index in range(graph_up.shape[0]):
        gathered = lax.all_gather(state, "vert", axis=1, tiled=True)
        summed = jax.vmap(aggregate)(gathered, tile_cols, blocks)
        graph_out = mlp_branch(
            state, summed, graph_gain[layer_index], graph_up[layer_index], graph_down[layer_index]
        )
        grouped = graph_out.reshape(snap_dev, owners, vert_dev // owners, feature_width)
        owned_rows = lax.all_to_all(grouped, "snap", split_axis=1, concat_axis=0, tiled=True)
        padded = jnp.concatenate(
            [jnp.zeros((lag_count - 1,) + owned_rows.shape[1:], jnp.bfloat16), owned_rows], axis=0
        )
        mixed_rows = lagged(padded, lag_mix[layer_index], lag_count - 1, owned_rows.shape[0])
        finished = mlp_branch(
            owned_rows,
            mixed_rows,
            time_gain[layer_index],
            time_up[layer_index],
            time_down[layer_index],
        )
        state = lax.all_to_all(finished, "snap", split_axis=0, concat_axis=1, tiled=True).reshape(
            snap_dev, vert_dev, feature_width
        )
    return state


def solution(mesh):
    return jax.shard_map(
        on_device,
        mesh=mesh,
        in_specs=(
            P("snap", "vert", None),
            P("snap", "vert", None),
            P("snap", "vert", None, None, None),
            P(),
            P(),
            P(),
            P(),
            P(),
            P(),
            P(),
        ),
        out_specs=P("snap", "vert", None),
        check_vma=False,
    )
```

profile of v0, /device:TPU:33, one launch (start us, length us, event | category | flops | bytes accessed | tf_op | source)
XLA Modules:
  0.0 265.1 jit_solution(5932802984013628403)
XLA Ops:
  6.5 0.0 all-gather.3.cloned.1.call-start
  6.5 0.7 all-gather.3.cloned.1.call-update
  7.3 0.7 fusion.81
  8.0 0.1 reshape.226
  8.0 0.8 slice_bitcast_fusion.9
  8.8 56.0 %all-gather.3.cloned.1.call-done = bf16[2,8192,128]{2,1,0:T(8,128)(2,1)} async-done(((bf16[2,1024,128]{2,1,0:T(8,128)(2,1)}), bf16[2,8192,128]{2,1,0:T(8,128)(2,1)}) %all-gather.3.cloned.1.call-update) | async-done | bytes 4194320 | tf_op jit(solution)/shard_map/all_gather | solution.py:66
  64.8 5.3 %gather_fusion = bf16[128,128,128]{2,1,0:T(8,128)(2,1)} fusion(bf16[2,64,128,128]{3,2,1,0:T(8,128)(2,1)} %bitcast.150, s32[128]{0:T(128)S(1)} %reshape.226), kind=kCustom, calls=%fused_computation | custom fusion | bytes 8389632 | tf_op jit(solution)/shard_map/vmap()/gather | solution.py:43
  70.1 5.9 %multiply_reduce_fusion.3 = (f32[2,8,128]{2,1,0:T(8,128)S(1)}, f32[2,8,128,128]{2,3,1,0:T(8,128)S(1)}) fusion(bf16[2,8,8,128,128]{4,3,2,1,0:T(8,128)(2,1)} %bitcast.143, s32[2,8,8,128,128]{4,3,2,1,0:T(8,128)} %param.12), kind=kOutput, calls=%fused_computation.91 | convolution fusion | flops 539490304 | bytes 13639680 | tf_op jit(solution)/shard_map/vmap(rkij,rkjf->rif)/dot_general | solution.py:44
  76.1 0.3 multiply_convert_fusion.3
  76.4 0.0 copy-start.1
  76.4 0.0 copy-start.3
  76.4 1.4 fusion.23
  77.9 0.0 copy-start.5
  77.9 0.0 copy-start.4
  77.9 0.0 copy-done.1
  77.9 0.0 copy-done.3
  77.9 0.7 fusion.42
  78.6 0.9 copy.19
  79.5 10.4 %all-to-all-start = ((bf16[2,32,32,128]{3,2,0,1:T(8,128)(2,1)}), bf16[2,32,32,128]{3,2,0,1:T(8,128)(2,1)S(1)}, u32[]{:S(2)}, u32[]{:S(2)}) async-start(bf16[2,32,32,128]{3,2,0,1:T(8,128)(2,1)} %copy.19), calls=%async_computation | async-start | bytes 1048576 | tf_op jit(solution)/shard_map/all_to_all | solution.py:72
  90.0 0.0 all-gather.5.cloned.1.call-start
  90.1 20.2 %all-to-all-done = bf16[2,32,32,128]{3,2,0,1:T(8,128)(2,1)S(1)} async-done(((bf16[2,32,32,128]{3,2,0,1:T(8,128)(2,1)}), bf16[2,32,32,128]{3,2,0,1:T(8,128)(2,1)S(1)}, u32[]{:S(2)}, u32[]{:S(2)}) %all-to-all-start) | async-done | bytes 524320 | tf_op jit(solution)/shard_map/all_to_all | solution.py:72
  110.3 0.1 pad_convert_fusion.1
  110.4 0.0 copy-start.6
  110.4 0.7 multiply_reduce_fusion.2
  111.1 0.3 multiply_convert_fusion.2
  111.5 0.0 copy-done.6
  111.5 0.0 copy-start.2
  111.5 2.9 %fusion.7 = bf16[2048,1024]{1,0:T(8,128)(2,1)S(1)} fusion(bf16[2048,128]{1,0:T(8,128)(2,1)S(1)} %bitcast.161, bf16[2,128,1024]{2,1,0:T(8,128)(2,1)S(1)} %copy-done.6), kind=kOutput, calls=%fused_computation.11 | convolution fusion | flops 555745280 | bytes 4980736 | tf_op jit(solution)/shard_map/dot_general | solution.py:20
  114.4 1.3 fusion.47
  115.7 21.4 %all_to_all.66 = bf16[64,1,32,128]{3,2,1,0:T(8,128)(2,1)S(1)} all-to-all(bf16[64,1,32,128]{3,2,1,0:T(8,128)(2,1)S(1)} %fusion.47), channel_id=1, replica_groups=mesh['snap'=32,'vert'=8] {'snap'}, dimensions={0} | all-to-all | bytes 1048576 | tf_op jit(solution)/shard_map/all_to_all | solution.py:84
  137.1 0.8 copy.21
  137.9 0.0 all-gather.5.cloned.1.call-update
  137.9 48.4 %all-gather.5.cloned.1.call-done = bf16[2,8192,128]{2,1,0:T(8,128)(2,1)} async-done(((bf16[2,1024,128]{2,1,0:T(8,128)(2,1)}), bf16[2,8192,128]{2,1,0:T(8,128)(2,1)}) %all-gather.5.cloned.1.call-update) | async-done | bytes 4194320 | tf_op jit(solution)/shard_map/all_gather | solution.py:66
  186.3 5.3 %gather_fusion.1 = bf16[128,128,128]{2,1,0:T(8,128)(2,1)} fusion(bf16[2,64,128,128]{3,2,1,0:T(8,128)(2,1)} %bitcast.151, s32[128]{0:T(128)S(1)} %reshape.226), kind=kCustom, calls=%fused_computation.1 | custom fusion | bytes 8389632 | tf_op jit(solution)/shard_map/vmap()/gather | solution.py:43
  191.6 5.9 %multiply_reduce_fusion.1 = (f32[2,8,128]{2,1,0:T(8,128)S(1)}, f32[2,8,128,128]{2,3,1,0:T(8,128)S(1)}) fusion(bf16[2,8,8,128,128]{4,3,2,1,0:T(8,128)(2,1)} %bitcast.142, s32[2,8,8,128,128]{4,3,2,1,0:T(8,128)} %param.12), kind=kOutput, calls=%fused_computation.87 | convolution fusion | flops 539490304 | bytes 13639680 | tf_op jit(solution)/shard_map/vmap(rkij,rkjf->rif)/dot_general | solution.py:44
  197.5 0.3 multiply_convert_fusion.1
  197.9 0.0 copy-start
  197.9 1.4 fusion.31
  199.3 0.7 fusion.43
  200.1 0.1 copy.22
  200.1 30.6 %all_to_all.67 = bf16[2,32,32,128]{3,2,0,1:T(8,128)(2,1)S(1)} all-to-all(bf16[2,32,32,128]{3,2,0,1:T(8,128)(2,1)S(1)} %copy.22), channel_id=1, replica_groups=mesh['snap'=32,'vert'=8] {'snap'}, dimensions={1} | all-to-all | bytes 1048576 | tf_op jit(solution)/shard_map/all_to_all | solution.py:72
  230.7 0.1 pad_convert_fusion
  230.8 0.7 multiply_reduce_fusion
  231.5 0.3 multiply_convert_fusion
  231.8 2.9 %fusion.15 = bf16[2048,1024]{1,0:T(8,128)(2,1)S(1)} fusion(bf16[2048,128]{1,0:T(8,128)(2,1)S(1)} %bitcast.163, bf16[2,128,1024]{2,1,0:T(8,128)(2,1)S(1)} %copy-done.6), kind=kOutput, calls=%fused_computation.19 | convolution fusion | flops 555745280 | bytes 4980736 | tf_op jit(solution)/shard_map/dot_general | solution.py:20
  234.8 1.3 fusion.46
  236.0 21.4 %all_to_all.68 = bf16[64,1,32,128]{3,2,1,0:T(8,128)(2,1)S(1)} all-to-all(bf16[64,1,32,128]{3,2,1,0:T(8,128)(2,1)S(1)} %fusion.46), channel_id=1, replica_groups=mesh['snap'=32,'vert'=8] {'snap'}, dimensions={0} | all-to-all | bytes 1048576 | tf_op jit(solution)/shard_map/all_to_all | solution.py:84
  257.4 0.8 copy.24
  (12 shorter events, 0.1 us)
Async XLA Ops:
  6.5 58.3 %all-gather.3.cloned.1.call-start = ((), (), s32[]{:S(2)}) async-start(), calls=%async_computation.4 | async-start | bytes 4718592 | tf_op jit(solution)/shard_map/all_gather | solution.py:66
  70.1 6.3 %copy-start.7 = (bf16[2,128,512]{2,1,0:T(8,128)(2,1)S(1)}, bf16[2,128,512]{2,1,0:T(8,128)(2,1)}, u32[]{:S(2)}) copy-start(bf16[2,128,512]{2,1,0:T(8,128)(2,1)} %param.14) | copy-start | bytes 786436
  76.4 1.5 copy-start.1
  76.4 1.5 copy-start.3
  77.9 12.1 %copy-start.5 = (f32[2,128]{1,0:T(2,128)S(1)}, f32[2,128]{1,0:T(2,128)}, u32[]{:S(2)}) copy-start(f32[2,128]{1,0:T(2,128)} %param.17) | copy-start | bytes 3076
  77.9 12.1 %copy-start.4 = (f32[2,8,128]{2,1,0:T(8,128)S(1)}, f32[2,8,128]{2,1,0:T(8,128)}, u32[]{:S(2)}) copy-start(f32[2,8,128]{2,1,0:T(8,128)} %param.16) | copy-start | bytes 24580
  79.5 30.8 %all-to-all-start = ((bf16[2,32,32,128]{3,2,0,1:T(8,128)(2,1)}), bf16[2,32,32,128]{3,2,0,1:T(8,128)(2,1)S(1)}, u32[]{:S(2)}, u32[]{:S(2)}) async-start(bf16[2,32,32,128]{3,2,0,1:T(8,128)(2,1)} %copy.19), calls=%async_computation | async-start | bytes 1048576 | tf_op jit(solution)/shard_map/all_to_all | solution.py:72
  90.0 96.4 %all-gather.5.cloned.1.call-start = ((), (), s32[]{:S(2)}) async-start(), calls=%async_computation.5 | async-start | bytes 4718592 | tf_op jit(solution)/shard_map/all_gather | solution.py:66
  110.4 1.0 copy-start.6
  111.5 3.0 %copy-start.2 = (bf16[2,1024,128]{2,1,0:T(8,128)(2,1)S(1)}, bf16[2,1024,128]{2,1,0:T(8,128)(2,1)}, u32[]{:S(2)}) copy-start(bf16[2,1024,128]{2,1,0:T(8,128)(2,1)} %param.19) | copy-start | bytes 1572868
  197.9 1.5 copy-start
Sparse Core Ops, SparseCore 0:
  9.1 55.6 all-gather.2
  138.1 48.2 all-gather.4
where the time goes:
time: 266 us; the launch traced here: 265 us
  waiting for transfers between devices  125 us (47%)
  blocking collectives  73.3 us (28%)
  matrix products  24.5 us (9%)
  local copies, waits for them, and re-layouts  14 us (5%)
  between operations  13.7 us (5%)
  starting transfers between devices  10.5 us (4%)
  other arithmetic  3.68 us (1%)
    all_gather x2, waiting for transfers between devices, on_device(): gathered = lax.all_gather(state, 'vert', axis=1, tiled=True)  104 us
    all_to_all x2, blocking collectives, on_device(): lax.all_to_all(finished, 'snap', split_axis=0, concat_axis=1, tiled=True)  42.8 us
    all_to_all x1, blocking collectives, on_device(): lax.all_to_all(grouped, 'snap', split_axis=1, concat_axis=0, tiled=True)  30.6 us
    all_to_all x1, waiting for transfers between devices, on_device(): lax.all_to_all(grouped, 'snap', split_axis=1, concat_axis=0, tiled=True)  20.2 us
    dot_general x2, matrix products, aggregate(): jnp.einsum('rkij,rkjf->rif', blocks, picked, preferred_element_type=jnp.f...  11.8 us
    gather x3, local copies, waits for them, and re-layouts, aggregate(): picked = stacked[columns]  10.6 us
    all_to_all x1, starting transfers between devices, on_device(): lax.all_to_all(grouped, 'snap', split_axis=1, concat_axis=0, tiled=True)  10.4 us
    dot_general x4, matrix products, mlp_branch(): jnp.dot(normed, up_weight, preferred_element_type=jnp.float32)  8.74 us
  transfers between devices with their start and end apart: 3, of which 3 were waited for; matrix products, arithmetic and copies ran while one was open for 1% of the time, Pallas kernels for 0%

commit v1 on v0

--- a/solution.py
+++ b/solution.py
@@ -63,7 +63,8 @@
     snap_dev, vert_dev, feature_width = features.shape
     lag_count = lag_mix.shape[1]
     for layer_index in range(graph_up.shape[0]):
-        gathered = lax.all_gather(state, "vert", axis=1, tiled=True)
+        repeated = jnp.stack([state] * lax.axis_size("vert"))
+        gathered = jnp.concatenate(lax.all_to_all(repeated, "vert", 0, 0), axis=1)
         summed = jax.vmap(aggregate)(gathered, tile_cols, blocks)
         graph_out = mlp_branch(
             state, summed, graph_gain[layer_index], graph_up[layer_index], graph_down[layer_index]

time: 266 us -> 347 us (1.30)
  the two profiles are of different devices: /device:TPU:33 before, /device:TPU:32 now
where the time goes in v1:
time: 347 us; the launch traced here: 346 us
  blocking collectives  167 us (48%)
  waiting for transfers between devices  108 us (31%)
  matrix products  24.5 us (7%)
  local copies, waits for them, and re-layouts  23.9 us (7%)
  starting transfers between devices  18.6 us (5%)
    all_to_all x1, blocking collectives, on_device(): gathered = jnp.concatenate(lax.all_to_all(repeated, 'vert', 0, 0), axis=1)  99.9 us
    all_to_all x1, waiting for transfers between devices, on_device(): gathered = jnp.concatenate(lax.all_to_all(repeated, 'vert', 0, 0), axis=1)  90.4 us
    all_to_all x2, blocking collectives, on_device(): lax.all_to_all(finished, 'snap', split_axis=0, concat_axis=1, tiled=True)  40.2 us
    all_to_all x1, blocking collectives, on_device(): lax.all_to_all(grouped, 'snap', split_axis=1, concat_axis=0, tiled=True)  27.4 us
    all_to_all x1, waiting for transfers between devices, on_device(): lax.all_to_all(grouped, 'snap', split_axis=1, concat_axis=0, tiled=True)  18 us
    all_to_all x1, starting transfers between devices, on_device(): lax.all_to_all(grouped, 'snap', split_axis=1, concat_axis=0, tiled=True)  12.2 us
    dot_general x2, matrix products, aggregate(): jnp.einsum('rkij,rkjf->rif', blocks, picked, preferred_element_type=jnp.f...  11.8 us
    gather x3, local copies, waits for them, and re-layouts, aggregate(): picked = stacked[columns]  10.6 us
  transfers between devices with their start and end apart: 2, of which 2 were waited for; matrix products, arithmetic and copies ran while one was open for 0% of the time, Pallas kernels for 0%

profile of v1, /device:TPU:32, one launch (start us, length us, event | category | flops | bytes accessed | tf_op | source)
XLA Modules:
  0.0 346.2 jit_solution(81291726882593230)
XLA Ops:
  0.0 3.8 %stack.4 = bf16[8,2,1024,128]{3,2,1,0:T(8,128)(2,1)} broadcast(bf16[2,1024,128]{2,1,0:T(8,128)(2,1)} %param.10), dimensions={1,2,3} | broadcast | bytes 4718592 | tf_op jit(solution)/shard_map/stack | solution.py:66
  3.8 6.4 %all-to-all-start = ((bf16[8,2,1024,128]{3,2,1,0:T(8,128)(2,1)}), bf16[8,2,1024,128]{3,2,1,0:T(8,128)(2,1)}, u32[]{:S(2)}, u32[]{:S(2)}) async-start(bf16[8,2,1024,128]{3,2,1,0:T(8,128)(2,1)} %stack.4), calls=%async_computation | async-start | bytes 8388608 | tf_op jit(solution)/shard_map/all_to_all | solution.py:67
  10.3 0.0 copy-done.3
  10.3 0.1 reshape.231
  10.4 0.0 copy-done.5
  10.4 90.4 %all-to-all-done = bf16[8,2,1024,128]{3,2,1,0:T(8,128)(2,1)} async-done(((bf16[8,2,1024,128]{3,2,1,0:T(8,128)(2,1)}), bf16[8,2,1024,128]{3,2,1,0:T(8,128)(2,1)}, u32[]{:S(2)}, u32[]{:S(2)}) %all-to-all-start) | async-done | bytes 4194336 | tf_op jit(solution)/shard_map/all_to_all | solution.py:67
  100.8 4.6 %copy.19 = bf16[8,2,1024,128]{3,2,0,1:T(8,128)(2,1)} copy(bf16[8,2,1024,128]{3,2,1,0:T(8,128)(2,1)} %all-to-all-done) | data formatting | bytes 8388608 | tf_op jit(solution)/shard_map/all_to_all | solution.py:67
  105.4 5.2 %gather_fusion = bf16[128,128,128]{2,1,0:T(8,128)(2,1)} fusion(bf16[2,64,128,128]{3,2,1,0:T(8,128)(2,1)} %bitcast.149, s32[128]{0:T(128)S(1)} %reshape.231), kind=kCustom, calls=%fused_computation | custom fusion | bytes 8389632 | tf_op jit(solution)/shard_map/vmap()/gather | solution.py:43
  110.6 5.9 %multiply_reduce_fusion.3 = (f32[2,8,128]{2,1,0:T(8,128)S(1)}, f32[2,8,128,128]{2,3,1,0:T(8,128)S(1)}) fusion(bf16[2,8,8,128,128]{4,3,2,1,0:T(8,128)(2,1)} %bitcast.147, s32[2,8,8,128,128]{4,3,2,1,0:T(8,128)} %param.12), kind=kOutput, calls=%fused_computation.91 | convolution fusion | flops 539490304 | bytes 13639680 | tf_op jit(solution)/shard_map/vmap(rkij,rkjf->rif)/dot_general | solution.py:44
  116.6 0.3 multiply_convert_fusion.3
  116.9 0.0 copy-done.8
  116.9 0.0 copy-start
  116.9 0.0 copy-start.2
  116.9 1.4 fusion.23
  118.4 0.0 copy-start.6
  118.4 0.0 copy-start.4
  118.4 0.7 fusion.42
  119.1 0.9 copy.20
  120.0 12.2 %all-to-all-start.1 = ((bf16[2,32,32,128]{3,2,0,1:T(8,128)(2,1)}), bf16[2,32,32,128]{3,2,0,1:T(8,128)(2,1)S(1)}, u32[]{:S(2)}, u32[]{:S(2)}) async-start(bf16[2,32,32,128]{3,2,0,1:T(8,128)(2,1)} %copy.20), calls=%async_computation.1 | async-start | bytes 1048576 | tf_op jit(solution)/shard_map/all_to_all | solution.py:73
  132.2 0.0 copy-done.6
  132.3 18.0 %all-to-all-done.1 = bf16[2,32,32,128]{3,2,0,1:T(8,128)(2,1)S(1)} async-done(((bf16[2,32,32,128]{3,2,0,1:T(8,128)(2,1)}), bf16[2,32,32,128]{3,2,0,1:T(8,128)(2,1)S(1)}, u32[]{:S(2)}, u32[]{:S(2)}) %all-to-all-start.1) | async-done | bytes 524320 | tf_op jit(solution)/shard_map/all_to_all | solution.py:73
  150.3 0.1 pad_convert_fusion.1
  150.4 0.0 copy-start.7
  150.4 0.7 multiply_reduce_fusion.2
  151.1 0.3 multiply_convert_fusion.2
  151.5 0.0 copy-done.7
  151.5 0.0 copy-start.1
  151.5 2.9 fusion.7
  154.4 0.0 copy-done.1
  154.4 1.3 fusion.47
  155.7 18.7 %all_to_all.76 = bf16[64,1,32,128]{3,2,1,0:T(8,128)(2,1)S(1)} all-to-all(bf16[64,1,32,128]{3,2,1,0:T(8,128)(2,1)S(1)} %fusion.47), channel_id=1, replica_groups=mesh['snap'=32,'vert'=8] {'snap'}, dimensions={0} | all-to-all | bytes 1048576 | tf_op jit(solution)/shard_map/all_to_all | solution.py:85
  174.5 0.8 stack.5
  175.3 99.9 %all_to_all.77 = bf16[8,2,1024,128]{3,2,1,0:T(8,128)(2,1)S(1)} all-to-all(bf16[8,2,1024,128]{3,2,1,0:T(8,128)(2,1)S(1)} %stack.5), channel_id=1, replica_groups=mesh['snap'=32,'vert'=8] {'vert'}, dimensions={0} | all-to-all | bytes 8388608 | tf_op jit(solution)/shard_map/all_to_all | solution.py:67
  275.2 2.2 copy.23
  277.4 5.3 %gather_fusion.1 = bf16[128,128,128]{2,1,0:T(8,128)(2,1)} fusion(bf16[2,64,128,128]{3,2,1,0:T(8,128)(2,1)} %bitcast.148, s32[128]{0:T(128)S(1)} %reshape.231), kind=kCustom, calls=%fused_computation.1 | custom fusion | bytes 8389632 | tf_op jit(solution)/shard_map/vmap()/gather | solution.py:43
  282.7 5.9 %multiply_reduce_fusion.1 = (f32[2,8,128]{2,1,0:T(8,128)S(1)}, f32[2,8,128,128]{2,3,1,0:T(8,128)S(1)}) fusion(bf16[2,8,8,128,128]{4,3,2,1,0:T(8,128)(2,1)} %bitcast.146, s32[2,8,8,128,128]{4,3,2,1,0:T(8,128)} %param.12), kind=kOutput, calls=%fused_computation.87 | convolution fusion | flops 539490304 | bytes 13639680 | tf_op jit(solution)/shard_map/vmap(rkij,rkjf->rif)/dot_general | solution.py:44
  288.6 0.3 multiply_convert_fusion.1
  289.0 1.4 fusion.31
  290.4 0.7 fusion.43
  291.1 0.1 copy.24
  291.2 27.4 %all_to_all.78 = bf16[2,32,32,128]{3,2,0,1:T(8,128)(2,1)S(1)} all-to-all(bf16[2,32,32,128]{3,2,0,1:T(8,128)(2,1)S(1)} %copy.24), channel_id=1, replica_groups=mesh['snap'=32,'vert'=8] {'snap'}, dimensions={1} | all-to-all | bytes 1048576 | tf_op jit(solution)/shard_map/all_to_all | solution.py:73
  318.5 0.1 pad_convert_fusion
  318.7 0.7 multiply_reduce_fusion
  319.4 0.3 multiply_convert_fusion
  319.7 2.9 fusion.15
  322.6 1.3 fusion.46
  323.9 21.4 %all_to_all.79 = bf16[64,1,32,128]{3,2,1,0:T(8,128)(2,1)S(1)} all-to-all(bf16[64,1,32,128]{3,2,1,0:T(8,128)(2,1)S(1)} %fusion.46), channel_id=1, replica_groups=mesh['snap'=32,'vert'=8] {'snap'}, dimensions={0} | all-to-all | bytes 1048576 | tf_op jit(solution)/shard_map/all_to_all | solution.py:85
  345.4 0.8 copy.26
  (15 shorter events, 0.1 us)
Async XLA Ops:
  3.8 6.4 %copy-start.3 = (s32[2,8,8]{2,1,0:T(8,128)S(1)}, s32[2,8,8]{2,1,0:T(8,128)}, u32[]{:S(2)}) copy-start(s32[2,8,8]{2,1,0:T(8,128)} %param.11) | copy-start | bytes 1540
  3.8 6.5 %copy-start.5 = (f32[2,128]{1,0:T(2,128)S(1)}, f32[2,128]{1,0:T(2,128)}, u32[]{:S(2)}) copy-start(f32[2,128]{1,0:T(2,128)} %param.13) | copy-start | bytes 3076
  3.8 96.9 %all-to-all-start = ((bf16[8,2,1024,128]{3,2,1,0:T(8,128)(2,1)}), bf16[8,2,1024,128]{3,2,1,0:T(8,128)(2,1)}, u32[]{:S(2)}, u32[]{:S(2)}) async-start(bf16[8,2,1024,128]{3,2,1,0:T(8,128)(2,1)} %stack.4), calls=%async_computation | async-start | bytes 8388608 | tf_op jit(solution)/shard_map/all_to_all | solution.py:67
  110.6 6.3 %copy-start.8 = (bf16[2,128,512]{2,1,0:T(8,128)(2,1)S(1)}, bf16[2,128,512]{2,1,0:T(8,128)(2,1)}, u32[]{:S(2)}) copy-start(bf16[2,128,512]{2,1,0:T(8,128)(2,1)} %param.14) | copy-start | bytes 786436
  116.9 1.5 copy-start
  116.9 1.5 copy-start.2
  118.4 13.8 %copy-start.6 = (f32[2,128]{1,0:T(2,128)S(1)}, f32[2,128]{1,0:T(2,128)}, u32[]{:S(2)}) copy-start(f32[2,128]{1,0:T(2,128)} %param.17) | copy-start | bytes 3076
  118.4 13.9 %copy-start.4 = (f32[2,8,128]{2,1,0:T(8,128)S(1)}, f32[2,8,128]{2,1,0:T(8,128)}, u32[]{:S(2)}) copy-start(f32[2,8,128]{2,1,0:T(8,128)} %param.16) | copy-start | bytes 24580
  120.0 30.3 %all-to-all-start.1 = ((bf16[2,32,32,128]{3,2,0,1:T(8,128)(2,1)}), bf16[2,32,32,128]{3,2,0,1:T(8,128)(2,1)S(1)}, u32[]{:S(2)}, u32[]{:S(2)}) async-start(bf16[2,32,32,128]{3,2,0,1:T(8,128)(2,1)} %copy.20), calls=%async_computation.1 | async-start | bytes 1048576 | tf_op jit(solution)/shard_map/all_to_all | solution.py:73
  150.4 1.0 copy-start.7
  151.5 2.9 copy-start.1
